TPU v7x, 256 devices: a whole 4x4x8 slice. The times are simulated.
256 devices in a mesh: src: 2 (over y_lo), tx: 8 (over y_hi, x), ty: 16 (over z, core).
Axes of the slice: x: 4, y: 4 (y_hi: 2, y_lo: 2; y = y_hi * 2 + y_lo), z: 8, core: 2. Of those that a mesh axis runs over, the one named last changes fastest.
Arguments:
- orders: float32 [8, 2, 512, 512], P('src', None, 'tx', 'ty'), may hold values from -0.00390625 to 0.00390625
- offsets: int32 [8, 2], P('src'), may hold values from -8 to 7
- material: int32 [6, 2048, 2048], P(None, 'tx', 'ty'), may hold values from 0 to 3
- e_field: float32 [3, 6, 2048, 2048], P(None, None, 'tx', 'ty'), may hold values from -6 to 6
- h_field: float32 [3, 6, 2048, 2048], P(None, None, 'tx', 'ty'), may hold values from -6 to 6
Outputs:
- e_out: float32 [3, 6, 2048, 2048], P(None, None, 'tx', 'ty')
- h_out: float32 [3, 6, 2048, 2048], P(None, None, 'tx', 'ty')
All inputs are finite; a program needn't handle non-finite values.
Results may differ from a plain program's by a relative error of at most 0.0003.
Values sent between devices are 32-bit elements; how exact they have to be, the bound alone decides.
A program may use at most 128 MiB of HBM per device.

v0:
```python
import math
import jax
import jax.numpy as jnp
from jax import lax
from jax.sharding import PartitionSpec as P

STEPS = 4
ZINJ = 1
COURANT = 0.5
OMEGA = 0.7
PERMITTIVITY = (1.0, 2.6, 11.9, 2.1)
PREC = lax.Precision.HIGH
SPLIT = 32


def passed_along(block, axis, distance):
    devices = range(lax.axis_size(axis))
    route = [((i - distance) % len(devices), i) for i in devices]
    return lax.ppermute(block, axis, route)


def phase_tables(freqs, positions, length):
    product = jnp.mod(freqs[:, None] * positions[None, :], length)
    angle = product.astype(jnp.float32) * (2.0 * math.pi / length)
    return (jnp.cos(angle), jnp.sin(angle))


def base_tables(orders_n, positions, length):
    hi = jnp.arange(orders_n // SPLIT, dtype=jnp.int32) * SPLIT
    lo = jnp.arange(SPLIT, dtype=jnp.int32) - orders_n // 2
    c1, s1 = phase_tables(hi, positions, length)
    c2, s2 = phase_tables(lo, positions, length)
    cos_t = c1[:, None, :] * c2[None, :, :] - s1[:, None, :] * s2[None, :, :]
    sin_t = s1[:, None, :] * c2[None, :, :] + c1[:, None, :] * s2[None, :, :]
    return (cos_t.reshape(orders_n, -1), sin_t.reshape(orders_n, -1))


def cell_coefficient(material):
    total = jnp.zeros(material.shape, jnp.float32)
    for number in range(len(PERMITTIVITY)):
        total = total + jnp.where(material == number, COURANT / PERMITTIVITY[number], 0.0)
    return total


def fwd(field, axis):
    if axis == 0:
        zero = jnp.zeros((1,) + field.shape[1:], jnp.float32)
        return jnp.concatenate([field[1:], zero], 0) - field
    return jnp.roll(field, -1, axis) - field


def bwd(field, axis):
    if axis == 0:
        zero = jnp.zeros((1,) + field.shape[1:], jnp.float32)
        return field - jnp.concatenate([zero, field[:-1]], 0)
    return field - jnp.roll(field, 1, axis)


def injection_plane(orders, offsets, cells_x, cells_y):
    points, _, rows_kx, cols_ky = orders.shape
    n_tx = lax.axis_size("tx")
    n_ty = lax.axis_size("ty")
    full_x = cells_x * n_tx
    full_y = cells_y * n_ty
    mx = rows_kx * n_tx
    my = cols_ky * n_ty
    amp = lax.all_gather(orders, "ty", axis=3, tiled=True)
    a_re = amp[:, 0]
    a_im = amp[:, 1]
    y_pos = lax.axis_index("ty") * cells_y + jnp.arange(cells_y, dtype=jnp.int32)
    by_c, by_s = base_tables(my, y_pos, full_y)
    sy_c, sy_s = phase_tables(offsets[:, 1], y_pos, full_y)
    m_re = jnp.einsum("pkj,jy->pky", a_re, by_c, precision=PREC) - jnp.einsum(
        "pkj,jy->pky", a_im, by_s, precision=PREC
    )
    m_im = jnp.einsum("pkj,jy->pky", a_re, by_s, precision=PREC) + jnp.einsum(
        "pkj,jy->pky", a_im, by_c, precision=PREC
    )
    sy_c = sy_c[:, None, :]
    sy_s = sy_s[:, None, :]
    inner = jnp.stack([m_re * sy_c - m_im * sy_s, m_re * sy_s + m_im * sy_c], 1)
    inner = lax.all_gather(inner, "tx", axis=2, tiled=True)
    i_re = inner[:, 0]
    i_im = inner[:, 1]
    x_pos = lax.axis_index("tx") * cells_x + jnp.arange(cells_x, dtype=jnp.int32)
    bx_c, bx_s = base_tables(mx, x_pos, full_x)
    sx_c, sx_s = phase_tables(offsets[:, 0], x_pos, full_x)
    q_re = jnp.einsum("kx,pky->pxy", bx_c, i_re, precision=PREC) - jnp.einsum(
        "kx,pky->pxy", bx_s, i_im, precision=PREC
    )
    q_im = jnp.einsum("kx,pky->pxy", bx_c, i_im, precision=PREC) + jnp.einsum(
        "kx,pky->pxy", bx_s, i_re, precision=PREC
    )
    sx_c = sx_c[:, :, None]
    sx_s = sx_s[:, :, None]
    plane = jnp.stack(
        [jnp.sum(q_re * sx_c - q_im * sx_s, 0), jnp.sum(q_re * sx_s + q_im * sx_c, 0)]
    )
    return lax.psum(plane, "src")


def with_halo(stack, depth):
    ahead = passed_along(stack[:, :depth], "tx", -1)
    behind = passed_along(stack[:, -depth:], "tx", 1)
    stack = jnp.concatenate([stack, ahead, behind], 1)
    ahead = passed_along(jnp.swapaxes(stack[:, :, :depth], 1, 2), "ty", -1)
    behind = passed_along(jnp.swapaxes(stack[:, :, -depth:], 1, 2), "ty", 1)
    return jnp.concatenate([stack, jnp.swapaxes(ahead, 1, 2), jnp.swapaxes(behind, 1, 2)], 2)


def per_device(orders, offsets, material, e_field, h_field):
    layers, cells_x, cells_y = material.shape
    plane = injection_plane(orders, offsets, cells_x, cells_y)
    coefficient = cell_coefficient(material)
    stack = jnp.concatenate(
        [
            e_field.reshape(3 * layers, cells_x, cells_y),
            h_field.reshape(3 * layers, cells_x, cells_y),
            coefficient,
            plane,
        ],
        0,
    )
    ext = with_halo(stack, STEPS)
    n = 3 * layers
    e_x, e_y, e_z = (ext[i * layers : (i + 1) * layers] for i in range(3))
    h_x, h_y, h_z = (ext[n + i * layers : n + (i + 1) * layers] for i in range(3))
    coefficient = ext[2 * n : 2 * n + layers]
    plane_re = ext[2 * n + layers]
    plane_im = ext[2 * n + layers + 1]
    for step in range(STEPS):
        h_x = h_x - COURANT * (fwd(e_z, 2) - fwd(e_y, 0))
        h_y = h_y - COURANT * (fwd(e_x, 0) - fwd(e_z, 1))
        h_z = h_z - COURANT * (fwd(e_y, 1) - fwd(e_x, 2))
        e_x = e_x + coefficient * (bwd(h_z, 2) - bwd(h_y, 0))
        e_y = e_y + coefficient * (bwd(h_x, 0) - bwd(h_z, 1))
        e_z = e_z + coefficient * (bwd(h_y, 1) - bwd(h_x, 2))
        cosine = math.cos(OMEGA * (step + 1))
        sine = math.sin(OMEGA * (step + 1))
        e_x = e_x.at[ZINJ].add(COURANT * (cosine * plane_re - sine * plane_im))
        e_y = e_y.at[ZINJ].add(COURANT * (sine * plane_re + cosine * plane_im))
    crop = lambda f: f[:, :cells_x, :cells_y]
    return (
        jnp.stack([crop(e_x), crop(e_y), crop(e_z)]),
        jnp.stack([crop(h_x), crop(h_y), crop(h_z)]),
    )


def solution(mesh):
    in_specs = (
        P("src", None, "tx", "ty"),
        P("src", None),
        P(None, "tx", "ty"),
        P(None, None, "tx", "ty"),
        P(None, None, "tx", "ty"),
    )
    out_specs = (P(None, None, "tx", "ty"), P(None, None, "tx", "ty"))
    return jax.shard_map(
        per_device, mesh=mesh, in_specs=in_specs, out_specs=out_specs, check_vma=False
    )
```

profile of v0, /device:TPU:1, one launch (start us, length us, event | category | flops | bytes accessed | tf_op | source)
XLA Modules:
  0.0 297.1 jit_solution(6683656501134292388)
XLA Ops:
  7.2 1.6 copy.27
  10.9 43.5 %all-gather.3.cloned.1.call-done = f32[4,2,64,512]{2,0,1,3:T(4,128)} async-done(((f32[4,2,64,32]{2,0,1,3:T(4,128)}), f32[4,2,64,512]{2,0,1,3:T(4,128)}) %all-gather.3.cloned.1.call-update) | async-done | bytes 1048592 | tf_op jit(solution)/shard_map/all_gather | solution.py:67
  54.4 1.7 fusion.128
  60.0 56.0 %all-gather.5.cloned.1.call-done = f32[4,2,512,128]{3,2,0,1:T(8,128)} async-done(((f32[4,2,64,128]{3,2,0,1:T(8,128)}), f32[4,2,512,128]{3,2,0,1:T(8,128)}) %all-gather.5.cloned.1.call-update) | async-done | bytes 2097168 | tf_op jit(solution)/shard_map/all_gather | solution.py:82
  116.0 2.4 fusion.75
  122.2 1.5 select_add_fusion
  123.7 33.4 %all-reduce.18.cloned.1.call-done = f32[2,256,128]{1,2,0:T(8,128)} async-done(((f32[2,256,128]{1,2,0:T(8,128)}), f32[2,256,128]{1,2,0:T(8,128)}) %all-reduce.18.cloned.1.call-update) | async-done | bytes 262160 | tf_op jit(solution)/shard_map/psum | solution.py:99
  159.3 4.6 %collective-permute-start = (f32[44,4,128]{2,1,0:T(4,128)S(1)}, f32[44,4,128]{2,1,0:T(4,128)S(1)}, u32[]{:S(2)}, u32[]{:S(2)}) collective-permute-start(f32[44,4,128]{2,1,0:T(4,128)S(1)} %get-tuple-element.134), channel_id=1, source_target_pairs={{16,0},{32,16},{48,32},{64,48},{80,64},{96,80},{112,96},{0,112},{1... | collective-permute-start | bytes 270344 | tf_op jit(solution)/shard_map/ppermute | solution.py:19
  163.9 1.6 collective-permute-done
  165.5 5.4 %collective-permute-done.1 = f32[44,4,128]{2,1,0:T(4,128)S(1)} collective-permute-done((f32[44,4,128]{2,1,0:T(4,128)S(1)}, f32[44,4,128]{2,1,0:T(4,128)S(1)}, u32[]{:S(2)}, u32[]{:S(2)}) %collective-permute-start.1) | collective-permute-done | bytes 90144 | tf_op jit(solution)/shard_map/ppermute | solution.py:19
  170.9 2.1 pad_maximum_fusion.1
  173.0 6.2 %slice_bitcast_fusion.1 = (f32[44,4,264]{1,2,0:T(8,128)}, f32[44,4,264]{1,2,0:T(8,128)}) fusion(f32[44,264,128]{2,1,0:T(8,128)S(1)} %pad_maximum_fusion.1), kind=kLoop, calls=%fused_computation.2 | loop fusion | bytes 743424 | tf_op jit(solution)/shard_map/transpose | solution.py:106
  179.2 5.5 %copy.35 = f32[44,4,264]{2,1,0:T(4,128)} copy(f32[44,4,264]{1,2,0:T(8,128)} %get-tuple-element.132) | data formatting | bytes 371712 | tf_op jit(solution)/shard_map/transpose | solution.py:106
  184.8 2.6 collective-permute-start.2
  187.3 5.5 %copy.37 = f32[44,4,264]{2,1,0:T(4,128)} copy(f32[44,4,264]{1,2,0:T(8,128)} %get-tuple-element.133) | data formatting | bytes 371712 | tf_op jit(solution)/shard_map/transpose | solution.py:107
  194.0 4.8 %copy.36 = f32[44,4,264]{1,2,0:T(8,128)} copy(f32[44,4,264]{2,1,0:T(4,128)} %collective-permute-done.2) | data formatting | bytes 371712 | tf_op jit(solution)/shard_map/ppermute | solution.py:19
  198.8 4.9 %copy.38 = f32[44,4,264]{1,2,0:T(8,128)} copy(f32[44,4,264]{2,1,0:T(4,128)} %collective-permute-done.3) | data formatting | bytes 371712 | tf_op jit(solution)/shard_map/ppermute | solution.py:19
  203.7 7.5 %pad_maximum_fusion = f32[44,264,136]{2,1,0:T(8,128)S(1)} fusion(f32[44,264,4]{2,1,0:T(8,128)} %bitcast.125, f32[44,264,4]{2,1,0:T(8,128)} %bitcast.124, f32[44,4,128]{2,1,0:T(4,128)} %copy-done.15, f32[44,4,128]{2,1,0:T(4,128)S(1)} %collective-permute-done, f32[2,256,128]{2,1,0:T(8,128)S(1)} %copy.34, f32[6,256,128]{2,1,0:T(8,128)S(1)} %select_add_fusion, ...), kind=kLoop, calls=%fused_computation | loop fusion | flops 11058432 | bytes 12638208 | tf_op jit(solution)/shard_map/concatenate | solution.py:108
  212.3 2.5 copy-done.3
  215.6 1.2 slice.667
  217.1 2.7 fusion.9
  221.5 2.3 fusion.17
  227.3 1.6 slice.660
  229.0 1.7 slice.673
  230.6 1.3 slice.669
  232.6 4.1 %fusion.20 = (f32[6,264,136]{2,1,0:T(8,128)S(1)}, f32[6,264,136]{2,1,0:T(8,128)S(1)}, f32[6,264,136]{2,1,0:T(8,128)S(1)}) fusion(f32[6,264,136]{2,1,0:T(8,128)S(1)} %get-tuple-element.122, f32[6,264,136]{2,1,0:T(8,128)S(1)} %get-tuple-element.120, f32[6,1,136]{2,1,0:T(1,128)S(1)} %slice.659, f32[6,263,136]{2,1,0:T(8,128)S(1)} %slice.658, ...), kind=kLoop, calls=%fused_computation.42 | loop fusion | flops 4093056 | bytes 12638208 | tf_op jit(solution)/shard_map/sub | solution.py:134
  236.8 1.2 slice.662
  239.1 1.2 slice.689
  241.5 3.5 %fusion.35 = (f32[6,264,136]{2,1,0:T(8,128)S(1)}, f32[6,264,136]{2,1,0:T(8,128)S(1)}, f32[6,264,136]{2,1,0:T(8,128)S(1)}) fusion(f32[6,264,136]{2,1,0:T(8,128)S(1)} %get-tuple-element.120, f32[6,264,136]{2,1,0:T(8,128)S(1)} %get-tuple-element.147, f32[6,263,136]{2,1,0:T(8,128)S(1)} %bitcast.108, f32[6,1,136]{2,1,0:T(1,128)S(1)} %slice.677, ...), kind=kLoop, calls=%fused_computation.64 | loop fusion | flops 4093056 | bytes 13499904 | tf_op jit(solution)/shard_map/add | solution.py:136
  247.2 1.2 slice.686
  248.5 1.6 slice.682
  250.2 1.7 slice.695
  251.8 1.3 slice.691
  253.1 4.1 %fusion.38 = (f32[6,264,136]{2,1,0:T(8,128)S(1)}, f32[6,264,136]{2,1,0:T(8,128)S(1)}, f32[6,264,136]{2,1,0:T(8,128)S(1)}) fusion(f32[6,264,136]{2,1,0:T(8,128)S(1)} %get-tuple-element.147, f32[6,264,136]{2,1,0:T(8,128)S(1)} %get-tuple-element.118, f32[6,1,136]{2,1,0:T(1,128)S(1)} %slice.681, f32[6,263,136]{2,1,0:T(8,128)S(1)} %slice.680, ...), kind=kLoop, calls=%fused_computation.68 | loop fusion | flops 4093056 | bytes 12638208 | tf_op jit(solution)/shard_map/sub | solution.py:134
  257.3 1.4 slice.684
  258.7 1.2 slice.693
  263.0 3.5 %fusion.53 = (f32[6,264,136]{2,1,0:T(8,128)S(1)}, f32[6,264,136]{2,1,0:T(8,128)S(1)}, f32[6,264,136]{2,1,0:T(8,128)S(1)}) fusion(f32[6,264,136]{2,1,0:T(8,128)S(1)} %get-tuple-element.118, f32[6,264,136]{2,1,0:T(8,128)S(1)} %get-tuple-element.144, f32[6,263,136]{2,1,0:T(8,128)S(1)} %bitcast.110, f32[6,1,136]{2,1,0:T(1,128)S(1)} %slice.699, ...), kind=kLoop, calls=%fused_computation.90 | loop fusion | flops 4093056 | bytes 13499904 | tf_op jit(solution)/shard_map/add | solution.py:136
  268.3 1.3 copy-done.6
  269.6 2.3 fusion.56
  271.9 1.4 slice.706
  273.4 1.2 slice.728
  274.6 1.2 slice.721
  276.5 5.5 %fusion.59 = (f32[6,264,136]{2,1,0:T(8,128)}, f32[6,264,136]{2,1,0:T(8,128)}, f32[6,264,136]{2,1,0:T(8,128)}) fusion(f32[6,264,136]{2,1,0:T(8,128)S(1)} %get-tuple-element.117, f32[6,264,136]{2,1,0:T(8,128)S(1)} %get-tuple-element.141, f32[6,264,135]{2,1,0:T(8,128)S(1)} %bitcast.117, f32[6,264,1]{2,1,0:T(8,128)} %slice.706, ...), kind=kLoop, calls=%fused_computation.99 | loop fusion | flops 2585088 | bytes 10914816 | tf_op jit(solution)/shard_map/add | solution.py:135
  282.0 2.1 fusion.87
  284.1 1.6 slice_bitcast_fusion.9
  285.7 1.7 slice_bitcast_fusion.11
  287.4 1.6 pad_maximum_fusion.3
  289.0 1.6 pad_maximum_fusion.2
  (115 shorter events, 31.4 us)
Async XLA Ops:
  7.2 47.2 %all-gather.3.cloned.1.call-start = ((), (), s32[]{:S(2)}) async-start(), calls=%async_computation | async-start | bytes 2228224 | tf_op jit(solution)/shard_map/all_gather | solution.py:67
  8.9 107.1 %all-gather.5.cloned.1.call-start = ((), (), s32[]{:S(2)}) async-start(), calls=%async_computation.1 | async-start | bytes 2359296 | tf_op jit(solution)/shard_map/all_gather | solution.py:82
  56.4 1.0 copy-start.14
  59.3 97.8 %all-reduce.18.cloned.1.call-start = ((), (), s32[]{:S(2)}) async-start(), calls=%async_computation.2 | async-start | bytes 524288 | tf_op jit(solution)/shard_map/psum | solution.py:99
  116.0 2.4 copy-start.11
  121.5 36.7 %copy-start.1 = (f32[3,6,256,128]{3,2,1,0:T(8,128)S(1)}, f32[3,6,256,128]{3,2,1,0:T(8,128)}, u32[]{:S(2)}) copy-start(f32[3,6,256,128]{3,2,1,0:T(8,128)} %param.25) | copy-start | bytes 7077892
  158.1 12.8 %copy-start.2 = (f32[3,6,256,128]{3,2,1,0:T(8,128)S(1)}, f32[3,6,256,128]{3,2,1,0:T(8,128)}, u32[]{:S(2)}) copy-start(f32[3,6,256,128]{3,2,1,0:T(8,128)} %param.24) | copy-start | bytes 7077892
  159.3 6.2 %collective-permute-start = (f32[44,4,128]{2,1,0:T(4,128)S(1)}, f32[44,4,128]{2,1,0:T(4,128)S(1)}, u32[]{:S(2)}, u32[]{:S(2)}) collective-permute-start(f32[44,4,128]{2,1,0:T(4,128)S(1)} %get-tuple-element.134), channel_id=1, source_target_pairs={{16,0},{32,16},{48,32},{64,48},{80,64},{96,80},{112,96},{0,112},{1... | collective-permute-start | bytes 270344 | tf_op jit(solution)/shard_map/ppermute | solution.py:19
  163.9 7.0 %collective-permute-start.1 = (f32[44,4,128]{2,1,0:T(4,128)S(1)}, f32[44,4,128]{2,1,0:T(4,128)S(1)}, u32[]{:S(2)}, u32[]{:S(2)}) collective-permute-start(f32[44,4,128]{2,1,0:T(4,128)S(1)} %get-tuple-element.135), channel_id=1, source_target_pairs={{112,0},{0,16},{16,32},{32,48},{48,64},{64,80},{80,96},{96,112},{1... | collective-permute-start | bytes 270344 | tf_op jit(solution)/shard_map/ppermute | solution.py:19
  170.9 2.1 copy-start.15
  184.8 9.2 %collective-permute-start.2 = (f32[44,4,264]{2,1,0:T(4,128)}, f32[44,4,264]{2,1,0:T(4,128)}, u32[]{:S(2)}, u32[]{:S(2)}) collective-permute-start(f32[44,4,264]{2,1,0:T(4,128)} %copy.35), channel_id=1, source_target_pairs={{1,0},{2,1},{3,2},{4,3},{5,4},{6,5},{7,6},{8,7},{9,8},{10,9},{11,1... | collective-permute-start | bytes 557576 | tf_op jit(solution)/shard_map/ppermute | solution.py:19
  192.8 6.0 %collective-permute-start.3 = (f32[44,4,264]{2,1,0:T(4,128)}, f32[44,4,264]{2,1,0:T(4,128)}, u32[]{:S(2)}, u32[]{:S(2)}) collective-permute-start(f32[44,4,264]{2,1,0:T(4,128)} %copy.37), channel_id=1, source_target_pairs={{15,0},{0,1},{1,2},{2,3},{3,4},{4,5},{5,6},{6,7},{7,8},{8,9},{9,10... | collective-permute-start | bytes 557576 | tf_op jit(solution)/shard_map/ppermute | solution.py:19
  211.2 55.4 %copy-start = (f32[44,264,136]{2,1,0:T(8,128)}, f32[44,264,136]{2,1,0:T(8,128)S(1)}, u32[]{:S(2)}) copy-start(f32[44,264,136]{2,1,0:T(8,128)S(1)} %pad_maximum_fusion) | copy-start | bytes 18957316
  211.4 3.4 %copy-start.3 = (f32[3,6,256,128]{3,2,1,0:T(8,128)S(1)}, f32[3,6,256,128]{3,2,1,0:T(8,128)}, u32[]{:S(2)}) copy-start(f32[3,6,256,128]{3,2,1,0:T(8,128)} %param.24) | copy-start | bytes 7077892
  211.4 3.4 %copy-start.16 = (f32[44,4,128]{2,1,0:T(4,128)S(1)}, f32[44,4,128]{2,1,0:T(4,128)}, u32[]{:S(2)}) copy-start(f32[44,4,128]{2,1,0:T(4,128)} %copy-done.15) | copy-start | bytes 270340
  219.8 1.2 copy-start.7
  220.1 1.4 copy-start.13
  230.6 2.0 copy-start.8
  257.3 2.7 copy-start.4
  261.1 1.9 copy-start.5
  268.1 1.4 copy-start.6
  271.9 1.5 copy-start.9
  274.6 1.9 copy-start.10
  284.1 1.6 copy-start.12
Sparse Core Ops, SparseCore 0:
  10.4 43.9 all-gather.2
  59.4 56.5 all-gather.4
  122.3 34.6 all-reduce.17
where the time goes:
time: 298 us; the launch traced here: 297 us
  waiting for transfers between devices  140 us (47%)
  local copies, waits for them, and re-layouts  75.9 us (25%)
  other arithmetic  51.6 us (17%)
  between operations  14.4 us (5%)
  starting transfers between devices  8.49 us (3%)
  matrix products  6.93 us (2%)
    all_gather x1, waiting for transfers between devices, injection_plane(): inner = lax.all_gather(inner, 'tx', axis=2, tiled=True)  56 us
    all_gather x1, waiting for transfers between devices, injection_plane(): amp = lax.all_gather(orders, 'ty', axis=3, tiled=True)  43.5 us
    psum x1, waiting for transfers between devices, injection_plane(): return lax.psum(plane, 'src')  33.4 us
    slice x27, local copies, waits for them, and re-layouts, fwd(): return jnp.roll(field, -1, axis) - field  15.9 us
    sub x4, other arithmetic, per_device(): h_z = h_z - COURANT * (fwd(e_y, 1) - fwd(e_x, 2))  13.2 us
    transpose x2, local copies, waits for them, and re-layouts, with_halo(): ahead = passed_along(jnp.swapaxes(stack[:, :, :depth], 1, 2), 'ty', -1)  11.7 us
    unnamed x37, local copies, waits for them, and re-layouts  9.9 us
    ppermute x2, local copies, waits for them, and re-layouts, passed_along(): return lax.ppermute(block, axis, route)  9.72 us
  transfers between devices with their start and end apart: 7, of which 5 were waited for; matrix products, arithmetic and copies ran while one was open for 5% of the time, Pallas kernels for 0%

commit v1 on v0

--- a/solution.py
+++ b/solution.py
@@ -96,7 +96,7 @@
     plane = jnp.stack(
         [jnp.sum(q_re * sx_c - q_im * sx_s, 0), jnp.sum(q_re * sx_s + q_im * sx_c, 0)]
     )
-    return lax.psum(plane, "src")
+    return jnp.sum(lax.all_gather(plane, "src"), axis=0)
 
 
 def with_halo(stack, depth):

time: 298 us -> 270 us (0.906)
  waiting for transfers between devices: 140 us -> 106 us
  blocking collectives: 0 us -> 6.6 us
    psum x1 -> x0, waiting for transfers between devices: 33.4 us -> none  [injection_plane(): return lax.psum(plane, 'src')]
    all_gather x0 -> x1, blocking collectives: none -> 6.6 us  [injection_plane(): return jnp.sum(lax.all_gather(plane, 'src'), axis=0)]
    unnamed x37 -> x39, local copies, waits for them, and re-layouts: 9.9 us -> 9.93 us
  transfers between devices with their start and end apart: 7 -> 6, of which waited for: 5 -> 4; matrix products, arithmetic and copies ran while one was open for 5% -> 5% of each run, Pallas kernels for 0% -> 0%
where the time goes in v1:
time: 270 us; the launch traced here: 269 us
  waiting for transfers between devices  106 us (39%)
  local copies, waits for them, and re-layouts  75.9 us (28%)
  other arithmetic  51.5 us (19%)
  between operations  14.7 us (5%)
  starting transfers between devices  7.72 us (3%)
  matrix products  6.92 us (3%)
  blocking collectives  6.6 us (2%)
    all_gather x1, waiting for transfers between devices, injection_plane(): inner = lax.all_gather(inner, 'tx', axis=2, tiled=True)  55.8 us
    all_gather x1, waiting for transfers between devices, injection_plane(): amp = lax.all_gather(orders, 'ty', axis=3, tiled=True)  43.5 us
    slice x27, local copies, waits for them, and re-layouts, fwd(): return jnp.roll(field, -1, axis) - field  15.8 us
    sub x4, other arithmetic, per_device(): h_z = h_z - COURANT * (fwd(e_y, 1) - fwd(e_x, 2))  13.2 us
    transpose x2, local copies, waits for them, and re-layouts, with_halo(): ahead = passed_along(jnp.swapaxes(stack[:, :, :depth], 1, 2), 'ty', -1)  11.7 us
    unnamed x39, local copies, waits for them, and re-layouts  9.93 us
    ppermute x2, local copies, waits for them, and re-layouts, passed_along(): return lax.ppermute(block, axis, route)  9.72 us
    add x3, other arithmetic, per_device(): e_y = e_y + coefficient * (bwd(h_x, 0) - bwd(h_z, 1))  9.23 us
  transfers between devices with their start and end apart: 6, of which 4 were waited for; matrix products, arithmetic and copies ran while one was open for 5% of the time, Pallas kernels for 0%

profile of v1, /device:TPU:1, one launch (start us, length us, event | category | flops | bytes accessed | tf_op | source)
XLA Modules:
  0.0 269.4 jit_solution(11153340789428831952)
XLA Ops:
  7.2 1.6 copy.27
  10.9 43.5 %all-gather.4.cloned.1.call-done = f32[4,2,64,512]{2,0,1,3:T(4,128)} async-done(((f32[4,2,64,32]{2,0,1,3:T(4,128)}), f32[4,2,64,512]{2,0,1,3:T(4,128)}) %all-gather.4.cloned.1.call-update) | async-done | bytes 1048592 | tf_op jit(solution)/shard_map/all_gather | solution.py:67
  54.4 1.7 fusion.128
  60.3 55.8 %all-gather.6.cloned.1.call-done = f32[4,2,512,128]{3,2,0,1:T(8,128)} async-done(((f32[4,2,64,128]{3,2,0,1:T(8,128)}), f32[4,2,512,128]{3,2,0,1:T(8,128)}) %all-gather.6.cloned.1.call-update) | async-done | bytes 2097168 | tf_op jit(solution)/shard_map/all_gather | solution.py:82
  116.0 2.4 fusion.75
  123.3 6.6 %all-gather = f32[4,256,128]{2,1,0:T(8,128)} all-gather(f32[2,256,128]{2,1,0:T(8,128)S(1)} %copy.34), channel_id=2, replica_groups=mesh['src'=2,'tx'=8,'ty'=16] {'src'}, dimensions={0}, use_global_device_ids=true | all-gather | bytes 786432 | tf_op jit(solution)/shard_map/all_gather | solution.py:99
  132.2 1.3 collective-permute-start
  133.7 1.9 collective-permute-done
  135.6 4.8 %collective-permute-done.1 = f32[44,4,128]{2,1,0:T(4,128)S(1)} collective-permute-done((f32[44,4,128]{2,1,0:T(4,128)S(1)}, f32[44,4,128]{2,1,0:T(4,128)S(1)}, u32[]{:S(2)}, u32[]{:S(2)}) %collective-permute-start.1) | collective-permute-done | bytes 90144 | tf_op jit(solution)/shard_map/ppermute | solution.py:19
  140.5 2.1 pad_maximum_fusion.1
  142.6 6.2 %slice_bitcast_fusion.1 = (f32[44,4,264]{1,2,0:T(8,128)}, f32[44,4,264]{1,2,0:T(8,128)}) fusion(f32[44,264,128]{2,1,0:T(8,128)S(1)} %pad_maximum_fusion.1), kind=kLoop, calls=%fused_computation.2 | loop fusion | bytes 743424 | tf_op jit(solution)/shard_map/transpose | solution.py:106
  148.8 5.5 %copy.35 = f32[44,4,264]{2,1,0:T(4,128)} copy(f32[44,4,264]{1,2,0:T(8,128)} %get-tuple-element.132) | data formatting | bytes 371712 | tf_op jit(solution)/shard_map/transpose | solution.py:106
  154.3 4.9 %collective-permute-start.2 = (f32[44,4,264]{2,1,0:T(4,128)}, f32[44,4,264]{2,1,0:T(4,128)}, u32[]{:S(2)}, u32[]{:S(2)}) collective-permute-start(f32[44,4,264]{2,1,0:T(4,128)} %copy.35), channel_id=1, source_target_pairs={{1,0},{2,1},{3,2},{4,3},{5,4},{6,5},{7,6},{8,7},{9,8},{10,9},{11,1... | collective-permute-start | bytes 557576 | tf_op jit(solution)/shard_map/ppermute | solution.py:19
  159.3 5.5 %copy.37 = f32[44,4,264]{2,1,0:T(4,128)} copy(f32[44,4,264]{1,2,0:T(8,128)} %get-tuple-element.133) | data formatting | bytes 371712 | tf_op jit(solution)/shard_map/transpose | solution.py:107
  164.8 1.2 collective-permute-start.3
  165.9 4.8 %copy.36 = f32[44,4,264]{1,2,0:T(8,128)} copy(f32[44,4,264]{2,1,0:T(4,128)} %collective-permute-done.2) | data formatting | bytes 371712 | tf_op jit(solution)/shard_map/ppermute | solution.py:19
  170.8 4.9 %copy.38 = f32[44,4,264]{1,2,0:T(8,128)} copy(f32[44,4,264]{2,1,0:T(4,128)} %collective-permute-done.3) | data formatting | bytes 371712 | tf_op jit(solution)/shard_map/ppermute | solution.py:19
  175.7 7.5 %pad_maximum_fusion = f32[44,264,136]{2,1,0:T(8,128)S(1)} fusion(f32[44,264,4]{2,1,0:T(8,128)} %bitcast.126, f32[44,264,4]{2,1,0:T(8,128)} %bitcast.125, f32[44,4,128]{2,1,0:T(4,128)} %copy-done.15, f32[44,4,128]{2,1,0:T(4,128)S(1)} %collective-permute-done, f32[2,256,128]{2,1,0:T(8,128)S(1)} %reduce_sum.35, f32[6,256,128]{2,1,0:T(8,128)S(1)} %select_add_fusion, ...), kind=kLoop, calls=%fused_computation | loop fusion | flops 11058432 | bytes 12638208 | tf_op jit(solution)/shard_map/concatenate | solution.py:108
  184.3 2.5 copy-done.3
  187.6 1.2 slice.667
  189.1 2.7 fusion.9
  193.5 2.3 fusion.17
  199.3 1.6 slice.660
  201.0 1.6 slice.673
  202.6 1.3 slice.669
  204.6 4.1 %fusion.20 = (f32[6,264,136]{2,1,0:T(8,128)S(1)}, f32[6,264,136]{2,1,0:T(8,128)S(1)}, f32[6,264,136]{2,1,0:T(8,128)S(1)}) fusion(f32[6,264,136]{2,1,0:T(8,128)S(1)} %get-tuple-element.122, f32[6,264,136]{2,1,0:T(8,128)S(1)} %get-tuple-element.120, f32[6,1,136]{2,1,0:T(1,128)S(1)} %slice.659, f32[6,263,136]{2,1,0:T(8,128)S(1)} %slice.658, ...), kind=kLoop, calls=%fused_computation.42 | loop fusion | flops 4093056 | bytes 12638208 | tf_op jit(solution)/shard_map/sub | solution.py:134
  208.7 1.2 slice.662
  211.1 1.2 slice.689
  213.5 3.5 %fusion.35 = (f32[6,264,136]{2,1,0:T(8,128)S(1)}, f32[6,264,136]{2,1,0:T(8,128)S(1)}, f32[6,264,136]{2,1,0:T(8,128)S(1)}) fusion(f32[6,264,136]{2,1,0:T(8,128)S(1)} %get-tuple-element.120, f32[6,264,136]{2,1,0:T(8,128)S(1)} %get-tuple-element.147, f32[6,263,136]{2,1,0:T(8,128)S(1)} %bitcast.109, f32[6,1,136]{2,1,0:T(1,128)S(1)} %slice.677, ...), kind=kLoop, calls=%fused_computation.64 | loop fusion | flops 4093056 | bytes 13499904 | tf_op jit(solution)/shard_map/add | solution.py:136
  219.2 1.2 slice.686
  220.5 1.6 slice.682
  222.1 1.7 slice.695
  223.8 1.3 slice.691
  225.1 4.1 %fusion.38 = (f32[6,264,136]{2,1,0:T(8,128)S(1)}, f32[6,264,136]{2,1,0:T(8,128)S(1)}, f32[6,264,136]{2,1,0:T(8,128)S(1)}) fusion(f32[6,264,136]{2,1,0:T(8,128)S(1)} %get-tuple-element.147, f32[6,264,136]{2,1,0:T(8,128)S(1)} %get-tuple-element.118, f32[6,1,136]{2,1,0:T(1,128)S(1)} %slice.681, f32[6,263,136]{2,1,0:T(8,128)S(1)} %slice.680, ...), kind=kLoop, calls=%fused_computation.68 | loop fusion | flops 4093056 | bytes 12638208 | tf_op jit(solution)/shard_map/sub | solution.py:134
  229.3 1.4 slice.684
  230.7 1.2 slice.693
  231.9 1.2 slice.711
  235.0 3.5 %fusion.53 = (f32[6,264,136]{2,1,0:T(8,128)S(1)}, f32[6,264,136]{2,1,0:T(8,128)S(1)}, f32[6,264,136]{2,1,0:T(8,128)S(1)}) fusion(f32[6,264,136]{2,1,0:T(8,128)S(1)} %get-tuple-element.118, f32[6,264,136]{2,1,0:T(8,128)S(1)} %get-tuple-element.144, f32[6,263,136]{2,1,0:T(8,128)S(1)} %bitcast.111, f32[6,1,136]{2,1,0:T(1,128)S(1)} %slice.699, ...), kind=kLoop, calls=%fused_computation.90 | loop fusion | flops 4093056 | bytes 13499904 | tf_op jit(solution)/shard_map/add | solution.py:136
  240.2 1.3 copy-done.6
  241.5 2.3 fusion.56
  243.9 1.4 slice.706
  245.4 1.2 slice.728
  248.5 5.5 %fusion.59 = (f32[6,264,136]{2,1,0:T(8,128)}, f32[6,264,136]{2,1,0:T(8,128)}, f32[6,264,136]{2,1,0:T(8,128)}) fusion(f32[6,264,136]{2,1,0:T(8,128)S(1)} %get-tuple-element.117, f32[6,264,136]{2,1,0:T(8,128)S(1)} %get-tuple-element.141, f32[6,264,135]{2,1,0:T(8,128)S(1)} %bitcast.118, f32[6,264,1]{2,1,0:T(8,128)} %slice.706, ...), kind=kLoop, calls=%fused_computation.99 | loop fusion | flops 2585088 | bytes 10914816 | tf_op jit(solution)/shard_map/add | solution.py:135
  253.9 2.1 fusion.87
  256.0 1.6 slice_bitcast_fusion.9
  257.7 1.7 slice_bitcast_fusion.11
  259.4 1.6 pad_maximum_fusion.3
  261.0 1.6 pad_maximum_fusion.2
  (116 shorter events, 31.9 us)
Async XLA Ops:
  7.2 47.2 %all-gather.4.cloned.1.call-start = ((), (), s32[]{:S(2)}) async-start(), calls=%async_computation | async-start | bytes 2228224 | tf_op jit(solution)/shard_map/all_gather | solution.py:67
  8.9 107.1 %all-gather.6.cloned.1.call-start = ((), (), s32[]{:S(2)}) async-start(), calls=%async_computation.1 | async-start | bytes 2359296 | tf_op jit(solution)/shard_map/all_gather | solution.py:82
  56.4 1.0 copy-start.14
  58.1 1.8 copy-start.17
  116.0 2.4 copy-start.11
  121.5 9.6 %copy-start.1 = (f32[3,6,256,128]{3,2,1,0:T(8,128)S(1)}, f32[3,6,256,128]{3,2,1,0:T(8,128)}, u32[]{:S(2)}) copy-start(f32[3,6,256,128]{3,2,1,0:T(8,128)} %param.25) | copy-start | bytes 7077892
  131.1 9.4 %copy-start.2 = (f32[3,6,256,128]{3,2,1,0:T(8,128)S(1)}, f32[3,6,256,128]{3,2,1,0:T(8,128)}, u32[]{:S(2)}) copy-start(f32[3,6,256,128]{3,2,1,0:T(8,128)} %param.24) | copy-start | bytes 7077892
  132.2 3.5 %collective-permute-start = (f32[44,4,128]{2,1,0:T(4,128)S(1)}, f32[44,4,128]{2,1,0:T(4,128)S(1)}, u32[]{:S(2)}, u32[]{:S(2)}) collective-permute-start(f32[44,4,128]{2,1,0:T(4,128)S(1)} %get-tuple-element.134), channel_id=1, source_target_pairs={{16,0},{32,16},{48,32},{64,48},{80,64},{96,80},{112,96},{0,112},{1... | collective-permute-start | bytes 270344 | tf_op jit(solution)/shard_map/ppermute | solution.py:19
  133.5 7.0 %collective-permute-start.1 = (f32[44,4,128]{2,1,0:T(4,128)S(1)}, f32[44,4,128]{2,1,0:T(4,128)S(1)}, u32[]{:S(2)}, u32[]{:S(2)}) collective-permute-start(f32[44,4,128]{2,1,0:T(4,128)S(1)} %get-tuple-element.135), channel_id=1, source_target_pairs={{112,0},{0,16},{16,32},{32,48},{48,64},{64,80},{80,96},{96,112},{1... | collective-permute-start | bytes 270344 | tf_op jit(solution)/shard_map/ppermute | solution.py:19
  140.5 2.1 copy-start.15
  154.3 11.6 %collective-permute-start.2 = (f32[44,4,264]{2,1,0:T(4,128)}, f32[44,4,264]{2,1,0:T(4,128)}, u32[]{:S(2)}, u32[]{:S(2)}) collective-permute-start(f32[44,4,264]{2,1,0:T(4,128)} %copy.35), channel_id=1, source_target_pairs={{1,0},{2,1},{3,2},{4,3},{5,4},{6,5},{7,6},{8,7},{9,8},{10,9},{11,1... | collective-permute-start | bytes 557576 | tf_op jit(solution)/shard_map/ppermute | solution.py:19
  164.8 6.0 %collective-permute-start.3 = (f32[44,4,264]{2,1,0:T(4,128)}, f32[44,4,264]{2,1,0:T(4,128)}, u32[]{:S(2)}, u32[]{:S(2)}) collective-permute-start(f32[44,4,264]{2,1,0:T(4,128)} %copy.37), channel_id=1, source_target_pairs={{15,0},{0,1},{1,2},{2,3},{3,4},{4,5},{5,6},{6,7},{7,8},{8,9},{9,10... | collective-permute-start | bytes 557576 | tf_op jit(solution)/shard_map/ppermute | solution.py:19
  183.2 55.4 %copy-start = (f32[44,264,136]{2,1,0:T(8,128)}, f32[44,264,136]{2,1,0:T(8,128)S(1)}, u32[]{:S(2)}) copy-start(f32[44,264,136]{2,1,0:T(8,128)S(1)} %pad_maximum_fusion) | copy-start | bytes 18957316
  183.4 3.4 %copy-start.3 = (f32[3,6,256,128]{3,2,1,0:T(8,128)S(1)}, f32[3,6,256,128]{3,2,1,0:T(8,128)}, u32[]{:S(2)}) copy-start(f32[3,6,256,128]{3,2,1,0:T(8,128)} %param.24) | copy-start | bytes 7077892
  183.4 3.4 %copy-start.16 = (f32[44,4,128]{2,1,0:T(4,128)S(1)}, f32[44,4,128]{2,1,0:T(4,128)}, u32[]{:S(2)}) copy-start(f32[44,4,128]{2,1,0:T(4,128)} %copy-done.15) | copy-start | bytes 270340
  191.8 1.2 copy-start.7
  192.1 1.4 copy-start.13
  202.6 2.0 copy-start.8
  229.2 2.7 copy-start.4
  233.1 1.9 copy-start.5
  240.1 1.4 copy-start.6
  243.8 1.5 copy-start.9
  246.6 1.9 copy-start.10
  256.0 1.6 copy-start.12
Sparse Core Ops, SparseCore 0:
  10.4 43.9 all-gather.3
  59.4 56.5 all-gather.5
